TPU v7x, 32 devices: a whole 2x2x4 slice. The times are simulated.
32 devices in a mesh: groups: 1, ctx: 2 (over x), fsdp: 16 (over z, y, core).
Axes of the slice: x: 2, y: 2, z: 4, core: 2. Of those that a mesh axis runs over, the one named last changes fastest.
Arguments:
- tokens: bfloat16 [16, 256, 3072], P(('groups', 'fsdp'), 'ctx'), may hold values from -600 to 600
- trace_index: int32 [16, 256], P(('groups', 'fsdp'), 'ctx'), may hold values from 0 to 1, never falling along the last dimension, each value on 1 to 192 neighbouring positions
- input_norm_scale: bfloat16 [3072], replicated, may hold values from 0.099609375 to 1.8984375
- query_weight: bfloat16 [3072, 2048], P('fsdp'), may hold values from -0.109375 to 0.109375
- key_weight: bfloat16 [3072, 1024], P('fsdp'), may hold values from -0.109375 to 0.109375
- value_weight: bfloat16 [3072, 1024], P('fsdp'), may hold values from -0.109375 to 0.109375
- query_down_weight: bfloat16 [3072, 16], replicated, may hold values from -0.109375 to 0.109375
- query_up_weight: bfloat16 [16, 2048], replicated, may hold values from -1.5 to 1.5
- value_down_weight: bfloat16 [3072, 16], replicated, may hold values from -0.109375 to 0.109375
- value_up_weight: bfloat16 [16, 1024], replicated, may hold values from -1.5 to 1.5
- output_gradient: bfloat16 [16, 256, 2048], P(('groups', 'fsdp'), 'ctx'), may hold values from -24 to 24
Outputs:
- grad_a_query: float32 [3072, 16], P('groups')
- grad_b_query: float32 [16, 2048], P('groups')
- grad_a_value: float32 [3072, 16], P('groups')
- grad_b_value: float32 [16, 1024], P('groups')
Inputs may be any that keep to these rules, and one draw needn't show every extreme that they name: `trace_index`: ids never fall along a sequence; one trace holds at most 192 positions.
All inputs are finite; a program needn't handle non-finite values.
Results may differ from a plain program's by a relative error of at most 0.013.
Values may be sent and summed in bfloat16 or wider, within the bound.
A program may use at most 128 MiB of HBM per device.

v0:
```python
import math

import jax
import jax.numpy as jnp
from jax import lax
from jax.sharding import PartitionSpec as P

HEAD_SIZE = 128


CAP = 50.0
QSCALE = 1.0 / 12.0
ADAPTER_NAME = 0.5
EPS = 1e-06


def shifted(value, axis, by):
    devices = lax.axis_size(axis)
    pairs = [(i, i + by) for i in range(devices) if 0 <= i + by < devices]
    return lax.ppermute(value, axis, pairs)


def normed_rows(values, gain):
    flt = values.astype(jnp.float32)
    meansq = jnp.mean(flt * flt, axis=-1, keepdims=True)
    return (flt * lax.rsqrt(meansq + EPS) * gain.astype(jnp.float32)).astype(jnp.bfloat16)


def add_rows(left, piece):
    return jnp.dot(left, piece, preferred_element_type=jnp.float32)


def attend_head(operands, mask):
    q_head, k_head, v_head, g_head = operands
    s = jnp.einsum("igd,jd->gij", q_head, k_head, preferred_element_type=jnp.float32) * QSCALE
    t = jnp.tanh(s / CAP)
    capped = CAP * t
    expo = jnp.where(mask[None], jnp.exp(capped), jnp.float32(0.0))
    weights = expo / jnp.sum(expo, axis=-1, keepdims=True)
    weights16 = weights.astype(jnp.bfloat16)
    attended = jnp.einsum("gij,jd->igd", weights16, v_head, preferred_element_type=jnp.float32)
    dweight = jnp.einsum("igd,jd->gij", g_head, v_head, preferred_element_type=jnp.float32)
    delta = jnp.sum(g_head.astype(jnp.float32) * attended, axis=-1).T
    dscore = (weights * (dweight - delta[..., None]) * (1.0 - t * t) * QSCALE).astype(jnp.bfloat16)
    query_gradient = jnp.einsum(
        "gij,jd->igd", dscore, k_head, preferred_element_type=jnp.float32
    ).astype(jnp.bfloat16)
    value_gradient = jnp.einsum(
        "gij,igd->jd", weights16, g_head, preferred_element_type=jnp.float32
    )
    return (query_gradient, value_gradient)


def partial_attend(mask):

    def run_head(operands):
        return attend_head(operands, mask)

    return run_head


def on_device(
    tokens,
    trace_index,
    input_norm_scale,
    query_weight,
    key_weight,
    value_weight,
    query_down_weight,
    query_up_weight,
    value_down_weight,
    value_up_weight,
    output_gradient,
):
    window_width = tokens.shape[1]
    feats = tokens.shape[2]
    heads_kv = key_weight.shape[1] // HEAD_SIZE
    heads_q = query_weight.shape[1] // HEAD_SIZE
    head_group = heads_q // heads_kv
    normalized_input = normed_rows(tokens.reshape(window_width, feats), input_norm_scale)
    seg_own = trace_index.reshape(window_width).astype(jnp.bfloat16)
    seg_parts = []

    def add_keyval(piece):
        return add_rows(normalized_input, piece)

    query_frozen = add_rows(
        normalized_input, lax.all_gather(query_weight, "fsdp", axis=0, tiled=True)
    )
    k_base = add_keyval(lax.all_gather(key_weight, "fsdp", axis=0, tiled=True))
    value_frozen = add_keyval(lax.all_gather(value_weight, "fsdp", axis=0, tiled=True))
    query_reduced = jnp.dot(
        normalized_input, query_down_weight, preferred_element_type=jnp.float32
    ).astype(jnp.bfloat16)
    reduced_rows = jnp.dot(
        normalized_input, value_down_weight, preferred_element_type=jnp.float32
    ).astype(jnp.bfloat16)
    query_matrix = (
        query_frozen
        + ADAPTER_NAME * jnp.dot(query_reduced, query_up_weight, preferred_element_type=jnp.float32)
    ).astype(jnp.bfloat16)
    key_rows = k_base.astype(jnp.bfloat16)
    value_rows = (
        value_frozen
        + ADAPTER_NAME * jnp.dot(reduced_rows, value_up_weight, preferred_element_type=jnp.float32)
    ).astype(jnp.bfloat16)
    key_parts = []
    value_parts = []
    for distance in (2, 1):
        key_prev, value_prev, seg_prev = shifted((key_rows, value_rows, seg_own), "ctx", distance)
        key_parts.append(key_prev)
        value_parts.append(value_prev)
        seg_parts.append(seg_prev)
    keys_all = jnp.concatenate(key_parts + [key_rows], 0)
    values_all = jnp.concatenate(value_parts + [value_rows], 0)
    seg_keys = jnp.concatenate(seg_parts + [seg_own], 0)
    pos_q = jnp.arange(window_width, dtype=jnp.int32)[:, None]
    pos_k = jnp.arange(3 * window_width, dtype=jnp.int32)[None, :]
    position = lax.axis_index("ctx")
    mask = (
        (pos_k > pos_q)
        & (pos_k <= pos_q + 2 * window_width)
        & (seg_keys[None, :] == seg_own[:, None])
    )
    mask = mask & (
        (pos_k >= 2 * window_width) | (pos_k >= window_width) & (position >= 1) | (position >= 2)
    )
    q_heads = jnp.moveaxis(
        query_matrix.reshape(window_width, heads_kv, head_group, HEAD_SIZE), 1, 0
    )
    g_heads = jnp.moveaxis(
        output_gradient.reshape(window_width, heads_kv, head_group, HEAD_SIZE), 1, 0
    )
    k_heads = jnp.moveaxis(keys_all.reshape(3 * window_width, heads_kv, HEAD_SIZE), 1, 0)
    v_heads = jnp.moveaxis(values_all.reshape(3 * window_width, heads_kv, HEAD_SIZE), 1, 0)
    dquery_heads, dvalue_heads = lax.map(partial_attend(mask), (q_heads, k_heads, v_heads, g_heads))
    query_gradient = jnp.moveaxis(dquery_heads, 0, 1).reshape(window_width, heads_q * HEAD_SIZE)
    dvalue_triple = jnp.moveaxis(dvalue_heads, 0, 1).reshape(3 * window_width, heads_kv * HEAD_SIZE)
    value_gradient = dvalue_triple[2 * window_width :]
    for distance in (1, 2):
        begin = (2 - distance) * window_width
        value_gradient = value_gradient + shifted(
            dvalue_triple[begin : begin + window_width], "ctx", -distance
        )
    query_backward = jnp.dot(
        query_gradient, query_up_weight.T, preferred_element_type=jnp.float32
    ).astype(jnp.bfloat16)
    value_backward = jnp.dot(
        value_gradient, value_up_weight.astype(jnp.float32).T, precision=lax.Precision.HIGHEST
    )
    part_aq = jnp.dot(normalized_input.T, query_backward, preferred_element_type=jnp.float32)
    part_bq = jnp.dot(query_reduced.T, query_gradient, preferred_element_type=jnp.float32)
    part_av = jnp.dot(
        normalized_input.astype(jnp.float32).T, value_backward, precision=lax.Precision.HIGHEST
    )
    part_bv = jnp.dot(
        reduced_rows.astype(jnp.float32).T, value_gradient, precision=lax.Precision.HIGHEST
    )
    sum_aq, sum_bq, sum_av, sum_bv = lax.psum((part_aq, part_bq, part_av, part_bv), ("ctx", "fsdp"))
    token_total = lax.axis_size("ctx") * lax.axis_size("fsdp") * window_width
    coefficient = ADAPTER_NAME / math.sqrt(token_total)
    return (sum_aq * coefficient, sum_bq * coefficient, sum_av * coefficient, sum_bv * coefficient)


def solution(mesh):
    return jax.shard_map(
        on_device,
        mesh=mesh,
        in_specs=(
            P(("groups", "fsdp"), "ctx", None),
            P(("groups", "fsdp"), "ctx"),
            P(),
            P("fsdp", None),
            P("fsdp", None),
            P("fsdp", None),
            P(),
            P(),
            P(),
            P(),
            P(("groups", "fsdp"), "ctx", None),
        ),
        out_specs=(P("groups", None), P("groups", None), P("groups", None), P("groups", None)),
        check_vma=False,
    )
```

profile of v0, /device:TPU:0, one launch (start us, length us, event | category | flops | bytes accessed | tf_op | source)
XLA Modules:
  0.0 444.9 jit_solution(15233795654485202083)
XLA Ops:
  12.4 62.1 %all-gather.8.cloned.1.call-done = bf16[3072,1024]{1,0:T(8,128)(2,1)} async-done(((bf16[192,1024]{1,0:T(8,128)(2,1)}), bf16[3072,1024]{1,0:T(8,128)(2,1)}) %all-gather.8.cloned.1.call-update) | async-done | bytes 6291472 | tf_op jit(solution)/shard_map/all_gather | solution.py:91
  74.5 3.8 fusion.71
  79.4 3.4 collective-permute-start.5
  82.8 54.1 %all-gather.4.cloned.1.call-done = bf16[3072,1024]{1,0:T(8,128)(2,1)} async-done(((bf16[192,1024]{1,0:T(8,128)(2,1)}), bf16[3072,1024]{1,0:T(8,128)(2,1)}) %all-gather.4.cloned.1.call-update) | async-done | bytes 6291472 | tf_op jit(solution)/shard_map/all_gather | solution.py:90
  136.9 3.8 convolution_convert_fusion
  141.4 4.1 collective-permute-start.1
  147.6 3.2 collective-permute-done.3
  151.0 2.0 bitcast_bitcast_fusion.1
  153.0 85.4 %all-gather.6.cloned.1.call-done = bf16[3072,2048]{1,0:T(8,128)(2,1)} async-done(((bf16[192,2048]{1,0:T(8,128)(2,1)}), bf16[3072,2048]{1,0:T(8,128)(2,1)}) %all-gather.6.cloned.1.call-update) | async-done | bytes 12582928 | tf_op jit(solution)/shard_map/all_gather | solution.py:88
  238.3 6.4 %fusion.74 = f32[128,2048]{1,0:T(8,128)S(1)} fusion(bf16[3072,2048]{1,0:T(8,128)(2,1)} %all-gather.6.cloned.1.call-done, bf16[1,128,3072]{2,1,0:T(8,128)(2,1)S(1)} %copy-done.1, f32[3072]{0:T(1024)S(1)} %convert_element_type.72, f32[128]{0:T(128)} %copy-done.14), kind=kOutput, calls=%fused_computation.95 | convolution fusion | flops 1612185600 | bytes 14430720 | tf_op jit(solution)/shard_map/dot_general | solution.py:30
  246.4 38.3 %while.15 = (s32[]{:T(128)}, bf16[8,128,2,128]{1,3,2,0:T(8,128)(2,1)}, f32[8,384,128]{1,2,0:T(8,128)}, bf16[8,384,128]{2,1,0:T(8,128)(2,1)}, bf16[8,128,2,128]{3...) while((s32[]{:T(128)}, ...), condition=%wide.region_4.5_spmd.clone, body=%wide.region_1.4_spmd.clone.sunk | while | flops 128122368 | bytes 3156989 | solution.py:136
  249.3 1.9 fusion.125
  254.1 1.9 fusion.125
  258.9 1.9 fusion.125
  263.7 1.9 fusion.125
  268.5 1.9 fusion.125
  273.3 1.9 fusion.125
  278.0 1.9 fusion.125
  282.8 1.9 fusion.125
  289.9 2.3 fusion.62
  292.2 10.1 %collective-permute-done.6 = f32[128,1024]{0,1:T(8,128)S(1)} collective-permute-done((f32[128,1024]{0,1:T(8,128)S(1)}, f32[128,1024]{0,1:T(8,128)S(1)}, u32[]{:S(2)}, u32[]{:S(2)}) %collective-permute-start.6) | collective-permute-done | bytes 524320 | tf_op jit(solution)/shard_map/ppermute | solution.py:20
  306.2 127.3 %all-reduce.3.cloned.1.call-done = (f32[3072,16]{0,1:T(8,128)}, f32[16,2048]{1,0:T(8,128)}, f32[3072,16]{0,1:T(8,128)}, f32[16,1024]{1,0:T(8,128)}) async-done(((f32[3072,16]{0,1:T(8,128)}, f32[16,2048]{1,0:T(8,128)}, f32[3072,16]{0,1:T(8,128)}, f32[16,1024]{1,0:T(8,128)}), (f32[3072,16]{0,1:T(8,128)}, f32[16,2048]{1,0:T(8,128)}, f32[3072,16]{0,1:T(8,128)}, ...) | async-done | bytes 589840 | tf_op jit(solution)/shard_map/psum | solution.py:159
  433.5 1.6 broadcast_multiply_fusion.2
  436.5 1.8 broadcast_multiply_fusion
  (138 shorter events, 44.0 us)
Async XLA Ops:
  7.2 3.8 copy-start
  7.2 67.2 %all-gather.8.cloned.1.call-start = ((), (), s32[]{:S(2)}) async-start(), calls=%async_computation.2 | async-start | bytes 6684672 | tf_op jit(solution)/shard_map/all_gather | solution.py:91
  7.9 128.9 %all-gather.4.cloned.1.call-start = ((), (), s32[]{:S(2)}) async-start(), calls=%async_computation | async-start | bytes 6684672 | tf_op jit(solution)/shard_map/all_gather | solution.py:90
  8.7 229.6 %all-gather.6.cloned.1.call-start = ((), (), s32[]{:S(2)}) async-start(), calls=%async_computation.1 | async-start | bytes 13369344 | tf_op jit(solution)/shard_map/all_gather | solution.py:88
  9.4 424.1 %all-reduce.3.cloned.1.call-start = ((), (), s32[]{:S(2)}) async-start(), calls=%async_computation.3 | async-start | bytes 1179648 | tf_op jit(solution)/shard_map/psum | solution.py:159
  9.5 141.3 %copy-start.6 = (bf16[128]{0:T(256)(128)(2,1)}, bf16[128]{0:T(256)(128)(2,1)S(1)}, u32[]{:S(2)}) copy-start(bf16[128]{0:T(256)(128)(2,1)S(1)} %convert_bitcast_fusion) | copy-start | bytes 772
  9.5 136.5 %collective-permute-start.2 = (bf16[128]{0:T(256)(128)(2,1)S(1)}, bf16[128]{0:T(256)(128)(2,1)S(1)}, u32[]{:S(2)}, u32[]{:S(2)}) collective-permute-start(bf16[128]{0:T(256)(128)(2,1)S(1)} %convert_bitcast_fusion), channel_id=1, source_target_pairs={} | collective-permute-start | bytes 776 | tf_op jit(solution)/shard_map/ppermute | solution.py:20
  11.0 125.9 %copy-start.14 = (f32[128]{0:T(128)}, f32[128]{0:T(128)S(1)}, u32[]{:S(2)}) copy-start(f32[128]{0:T(128)S(1)} %add_rsqrt_fusion) | copy-start | bytes 1540
  11.3 66.9 %copy-start.8 = (bf16[128,16]{0,1:T(8,128)(2,1)}, bf16[128,16]{0,1:T(8,128)(2,1)S(1)}, u32[]{:S(2)}) copy-start(bf16[128,16]{0,1:T(8,128)(2,1)S(1)} %convolution_convert_fusion.2) | copy-start | bytes 12292
  12.4 65.9 %copy-start.4 = (bf16[16,1024]{1,0:T(8,128)(2,1)S(1)}, bf16[16,1024]{1,0:T(8,128)(2,1)}, u32[]{:S(2)}) copy-start(bf16[16,1024]{1,0:T(8,128)(2,1)} %param.22) | copy-start | bytes 98308
  78.5 68.8 %copy-start.3 = (bf16[1,128,2048]{2,1,0:T(8,128)(2,1)S(1)}, bf16[1,128,2048]{2,1,0:T(8,128)(2,1)}, u32[]{:S(2)}) copy-start(bf16[1,128,2048]{2,1,0:T(8,128)(2,1)} %param.23) | copy-start | bytes 1572868
  78.6 72.2 %collective-permute-start.4 = (bf16[128,1024]{1,0:T(8,128)(2,1)S(1)}, bf16[128,1024]{1,0:T(8,128)(2,1)S(1)}, u32[]{:S(2)}, u32[]{:S(2)}) collective-permute-start(bf16[128,1024]{1,0:T(8,128)(2,1)S(1)} %fusion.61), channel_id=1, source_target_pairs={} | collective-permute-start | bytes 786440 | tf_op jit(solution)/shard_map/ppermute | solution.py:20
  79.4 71.4 %collective-permute-start.5 = (bf16[128,1024]{1,0:T(8,128)(2,1)S(1)}, bf16[128,1024]{1,0:T(8,128)(2,1)S(1)}, u32[]{:S(2)}, u32[]{:S(2)}) collective-permute-start(bf16[128,1024]{1,0:T(8,128)(2,1)S(1)} %fusion.61), channel_id=1, source_target_pairs={{0,16},{1,17},{2,18},{3,19},{4,20},{5,21},{6,22},{7,23},{8,24},{9,... | collective-permute-start | bytes 786440 | tf_op jit(solution)/shard_map/ppermute | solution.py:20
  140.7 10.2 %collective-permute-start = (bf16[128,1024]{1,0:T(8,128)(2,1)S(1)}, bf16[128,1024]{1,0:T(8,128)(2,1)S(1)}, u32[]{:S(2)}, u32[]{:S(2)}) collective-permute-start(bf16[128,1024]{1,0:T(8,128)(2,1)S(1)} %convolution_convert_fusion), channel_id=1, source_target_pairs={} | collective-permute-start | bytes 786440 | tf_op jit(solution)/shard_map/ppermute | solution.py:20
  141.4 9.6 %collective-permute-start.1 = (bf16[128,1024]{1,0:T(8,128)(2,1)S(1)}, bf16[128,1024]{1,0:T(8,128)(2,1)}, u32[]{:S(2)}, u32[]{:S(2)}) collective-permute-start(bf16[128,1024]{1,0:T(8,128)(2,1)S(1)} %convolution_convert_fusion), channel_id=1, source_target_pairs={{0,16},{1,17},{2,18},{3,19},{4,20},{5,21},{6,22},{7,23},{8,24},{9,... | collective-permute-start | bytes 786440 | tf_op jit(solution)/shard_map/ppermute | solution.py:20
  146.0 4.8 %collective-permute-start.3 = (bf16[128]{0:T(256)(128)(2,1)S(1)}, bf16[128]{0:T(256)(128)(2,1)S(1)}, u32[]{:S(2)}, u32[]{:S(2)}) collective-permute-start(bf16[128]{0:T(256)(128)(2,1)S(1)} %convert_bitcast_fusion), channel_id=1, source_target_pairs={{0,16},{1,17},{2,18},{3,19},{4,20},{5,21},{6,22},{7,23},{8,24},{9,... | collective-permute-start | bytes 776 | tf_op jit(solution)/shard_map/ppermute | solution.py:20
  153.0 91.8 %copy-start.5 = (bf16[16,2048]{1,0:T(8,128)(2,1)S(1)}, bf16[16,2048]{1,0:T(8,128)(2,1)}, u32[]{:S(2)}) copy-start(bf16[16,2048]{1,0:T(8,128)(2,1)} %param.20) | copy-start | bytes 196612
  153.0 91.8 %copy-start.10 = (bf16[128,16]{0,1:T(8,128)(2,1)S(1)}, bf16[128,16]{0,1:T(8,128)(2,1)}, u32[]{:S(2)}) copy-start(bf16[128,16]{0,1:T(8,128)(2,1)} %convolution_convert_fusion.3) | copy-start | bytes 12292
  284.7 4.3 copy-start.2
  284.7 4.3 copy-start.11
  284.7 5.2 %copy-start.15 = (f32[128]{0:T(128)S(1)}, f32[128]{0:T(128)}, u32[]{:S(2)}) copy-start(f32[128]{0:T(128)} %copy-done.14) | copy-start | bytes 1540
  286.3 16.0 %collective-permute-start.6 = (f32[128,1024]{0,1:T(8,128)S(1)}, f32[128,1024]{0,1:T(8,128)S(1)}, u32[]{:S(2)}, u32[]{:S(2)}) collective-permute-start(f32[128,1024]{0,1:T(8,128)S(1)} %bitcast.193), channel_id=1, source_target_pairs={{16,0},{17,1},{18,2},{19,3},{20,4},{21,5},{22,6},{23,7},{24,8},{25... | collective-permute-start | bytes 1572872 | tf_op jit(solution)/shard_map/ppermute | solution.py:20
  287.6 14.7 %collective-permute-start.7 = (f32[128,1024]{0,1:T(8,128)S(1)}, f32[128,1024]{0,1:T(8,128)}, u32[]{:S(2)}, u32[]{:S(2)}) collective-permute-start(f32[128,1024]{0,1:T(8,128)S(1)} %bitcast.192), channel_id=1, source_target_pairs={} | collective-permute-start | bytes 1572872 | tf_op jit(solution)/shard_map/ppermute | solution.py:20
  292.2 11.8 %copy-start.9 = (bf16[128,16]{0,1:T(8,128)(2,1)S(1)}, bf16[128,16]{0,1:T(8,128)(2,1)}, u32[]{:S(2)}) copy-start(bf16[128,16]{0,1:T(8,128)(2,1)} %copy-done.8) | copy-start | bytes 12292
  (7 other events, 16.4 us)
Sparse Core Ops, SparseCore 0:
  10.3 64.1 all-gather.7
  76.7 60.0 all-gather.3
  139.2 99.1 all-gather.5
  306.4 127.0 all-reduce.2
where the time goes:
time: 446 us; the launch traced here: 445 us
  waiting for transfers between devices  344 us (77%)
  matrix products  57 us (13%)
  between operations  14.1 us (3%)
  starting transfers between devices  13.8 us (3%)
  other arithmetic  11.5 us (3%)
    psum x1, waiting for transfers between devices, on_device(): lax.psum((part_aq, part_bq, part_av, part_bv), ('ctx', 'fsdp'))  127 us
    all_gather x1, waiting for transfers between devices, on_device(): lax.all_gather(query_weight, 'fsdp', axis=0, tiled=True)  85.4 us
    all_gather x1, waiting for transfers between devices, on_device(): lax.all_gather(value_weight, 'fsdp', axis=0, tiled=True)  62.1 us
    all_gather x1, waiting for transfers between devices, on_device(): k_base = add_keyval(lax.all_gather(key_weight, 'fsdp', axis=0, tiled=True))  54.1 us
    dot_general x8, matrix products, attend_head(): jnp.einsum('gij,jd->igd', dscore, k_head, preferred_element_type=jnp.floa...  15.3 us
    dot_general x3, matrix products, add_rows(): return jnp.dot(left, piece, preferred_element_type=jnp.float32)  14.1 us
    ppermute x8, starting transfers between devices, shifted(): return lax.ppermute(value, axis, pairs)  13.6 us
    ppermute x8, waiting for transfers between devices, shifted(): return lax.ppermute(value, axis, pairs)  13.2 us
  transfers between devices with their start and end apart: 12, of which 6 were waited for; matrix products, arithmetic and copies ran while one was open for 4% of the time, Pallas kernels for 0%

commit v1 on v0

--- a/solution.py
+++ b/solution.py
@@ -1,8 +1,11 @@
+import functools
 import math
 
 import jax
 import jax.numpy as jnp
 from jax import lax
+from jax.experimental import pallas as pl
+from jax.experimental.pallas import tpu as pltpu
 from jax.sharding import PartitionSpec as P
 
 HEAD_SIZE = 128
@@ -162,9 +165,431 @@
     return (sum_aq * coefficient, sum_bq * coefficient, sum_av * coefficient, sum_bv * coefficient)
 
 
+F32 = jnp.float32
+BF16 = jnp.bfloat16
+PLANE = 8
+
+
+def dot(a, b, dims=((1,), (0,))):
+    return lax.dot_general(a, b, (dims, ((), ())), preferred_element_type=F32)
+
+
+def plane_kernel(
+    chain, coefficient,
+    norm, seg, wq, wk, wv, qd, qu, vd, vu, grad,
+    out_aq, out_bq, out_av, out_bv,
+    N, W, G, SG, acc, DQ, DV, LQ, LV, A, RA, S, RS, T, OUT,
+    local_sem, w_send, w_recv, t_send, t_recv, g_send, g_recv, s_send, s_recv,
+    up_send, up_recv, down_send, down_recv,
+    r1_send, r1_recv, r2_send, r2_recv, r3_send, r3_recv,
+):
+    x = lax.axis_index("ctx")
+    f = lax.axis_index("fsdp")
+    z = f // 4
+    y = (f // 2) % 2
+    c = f % 2
+    tok, feats = norm.shape
+    rows = wq.shape[0]
+    qcols = wq.shape[1] // PLANE
+    kcols = wk.shape[1] // PLANE
+    piece = feats // PLANE
+    plane_rows = 4 * rows
+    seq = 2 * tok
+
+    def coords(r):
+        px = 1 - x if r & 4 else x
+        py = 1 - y if r & 2 else y
+        pc = 1 - c if r & 1 else c
+        return px, py, pc
+
+    def head_of(r):
+        px, py, pc = coords(r)
+        return (px * 2 + py) * 2 + pc
+
+    def peer(r):
+        px, py, pc = coords(r)
+        return {"ctx": px, "fsdp": (z * 2 + py) * 2 + pc}
+
+    def above(pz):
+        return {"ctx": x, "fsdp": (pz * 2 + y) * 2 + c}
+
+    def tok_rows(r):
+        px, py, pc = coords(r)
+        return pl.ds(pl.multiple_of(((py * 2 + pc) * 2 + px) * tok, tok), tok)
+
+    def remote(src, dst, send, recv, device):
+        return pltpu.make_async_remote_copy(
+            src_ref=src, dst_ref=dst, send_sem=send, recv_sem=recv,
+            device_id=device, device_id_type=pl.DeviceIdType.MESH,
+        )
+
+    barrier = pltpu.get_barrier_semaphore()
+    for r in range(1, PLANE):
+        pl.semaphore_signal(barrier, inc=1, device_id=peer(r), device_id_type=pl.DeviceIdType.MESH)
+    for d in range(1, chain):
+        pl.semaphore_signal(
+            barrier, inc=1, device_id=above((z + d) % chain), device_id_type=pl.DeviceIdType.MESH
+        )
+
+    def w_rows(r):
+        px, py, pc = coords(r)
+        return pl.ds(pl.multiple_of(((z * 2 + py) * 2 + pc) * rows, rows), rows)
+
+    def w_parts(r):
+        h = head_of(r)
+        own = w_rows(0)
+        return (
+            (wq.at[:, pl.ds(pl.multiple_of(h * qcols, qcols), qcols)], W.at[own, pl.ds(0, qcols)]),
+            (wk.at[:, pl.ds(pl.multiple_of(h * kcols, kcols), kcols)], W.at[own, pl.ds(qcols, kcols)]),
+            (wv.at[:, pl.ds(pl.multiple_of(h * kcols, kcols), kcols)], W.at[own, pl.ds(qcols + kcols, kcols)]),
+        )
+
+    def g_cols(r):
+        h = head_of(r)
+        return grad.at[:, pl.ds(pl.multiple_of(h * qcols, qcols), qcols)]
+
+    local = [pltpu.make_async_copy(a, b, local_sem.at[i]) for i, (a, b) in enumerate(w_parts(0))]
+    local.append(pltpu.make_async_copy(norm, N.at[tok_rows(0)], local_sem.at[3]))
+    local.append(pltpu.make_async_copy(g_cols(0), G.at[tok_rows(0)], local_sem.at[4]))
+    local.append(pltpu.make_async_copy(seg, SG.at[tok_rows(0)], local_sem.at[5]))
+    for copy in local:
+        copy.start()
+    pl.semaphore_wait(barrier, PLANE - 1 + chain - 1)
+
+    w_copies = {}
+    for r in (1, 2, 3):
+        w_copies[r] = [
+            remote(a, b, w_send.at[r, i], w_recv.at[r, i], peer(r)) for i, (a, b) in enumerate(w_parts(r))
+        ]
+        for copy in w_copies[r]:
+            copy.start()
+    t_copies = {}
+    for r in (2, 4, 1):
+        t_copies[r] = remote(norm, N.at[tok_rows(0)], t_send.at[r], t_recv.at[r], peer(r))
+        t_copies[r].start()
+    g_copies = {}
+    s_copies = {}
+    for r in range(1, PLANE):
+        g_copies[r] = remote(g_cols(r), G.at[tok_rows(0)], g_send.at[r], g_recv.at[r], peer(r))
+        s_copies[r] = remote(seg, SG.at[tok_rows(0)], s_send.at[r], s_recv.at[r], peer(r))
+
+    def half_rows(plane, half):
+        py = y if half == 0 else 1 - y
+        return pl.ds(pl.multiple_of((plane * 4 + py * 2) * rows, 2 * rows), 2 * rows)
+
+    def up_copy(t, half):
+        at = W.at[half_rows(z - t, half)]
+        return remote(at, at, up_send.at[t, half], up_recv.at[t, half], above(z + 1))
+
+    def down_copy(t, half):
+        at = W.at[half_rows(z + t, half)]
+        return remote(at, at, down_send.at[t, half], down_recv.at[t, half], above(z - 1))
+
+    def up_arrival(t, half):
+        at = W.at[half_rows(z - 1 - t, half)]
+        return remote(at, at, up_send.at[t, half], up_recv.at[t, half], above(z - 1))
+
+    def down_arrival(t, half):
+        at = W.at[half_rows(z + 1 + t, half)]
+        return remote(at, at, down_send.at[t, half], down_recv.at[t, half], above(z + 1))
+
+    def has_up(t):
+        return (z < chain - 1) & (z - t >= 0)
+
+    def has_down(t):
+        return (z > 0) & (z + t <= chain - 1)
+
+    def send_chain(t, half):
+        @pl.when(has_up(t))
+        def _():
+            up_copy(t, half).start()
+
+        @pl.when(has_down(t))
+        def _():
+            down_copy(t, half).start()
+
+    def recv_chain(t, half):
+        @pl.when(z - 1 - t >= 0)
+        def _():
+            up_arrival(t, half).wait_recv()
+
+        @pl.when(z + 1 + t <= chain - 1)
+        def _():
+            down_arrival(t, half).wait_recv()
+
+    def forward_token(r_mine, r_there, hop):
+        at = N.at[tok_rows(r_mine)]
+        t_copies[r_there] = remote(at, at, t_send.at[r_there], t_recv.at[r_there], peer(hop))
+        t_copies[r_there].start()
+
+    def wait_token(r):
+        at = N.at[tok_rows(r)]
+        remote(at, at, t_send.at[r], t_recv.at[r], peer(1)).wait_recv()
+
+    def wait_weight(r):
+        at = w_rows(r)
+        for i, (lo, width) in enumerate(((0, qcols), (qcols, kcols), (qcols + kcols, kcols))):
+            ref = W.at[at, pl.ds(lo, width)]
+            remote(ref, ref, w_send.at[r, i], w_recv.at[r, i], peer(r)).wait_recv()
+
+    for i in range(3):
+        local[i].wait()
+    wait_weight(1)
+    send_chain(0, 0)
+    wait_weight(2)
+    wait_weight(3)
+    send_chain(0, 1)
+    for r in range(1, PLANE):
+        g_copies[r].start()
+        s_copies[r].start()
+    wait_token(4)
+    forward_token(4, 5, 1)
+    if chain > 1:
+        for half in range(2):
+            recv_chain(0, half)
+            if chain > 2:
+                send_chain(1, half)
+    wait_token(2)
+    forward_token(2, 6, 4)
+    forward_token(2, 3, 1)
+    for t in range(1, chain - 2):
+        for half in range(2):
+            recv_chain(t, half)
+            send_chain(t + 1, half)
+    wait_token(6)
+    forward_token(6, 7, 1)
+    local[3].wait()
+    for r in (1, 5, 3, 7):
+        wait_token(r)
+
+    tiles = PLANE * tok // seq
+
+    @pl.loop(0, tiles)
+    def _(i):
+        at = pl.ds(pl.multiple_of(i * seq, seq), seq)
+        block = N[at, :]
+        LQ[at, :] = dot(block, qd[...]).astype(BF16)
+        LV[at, :] = dot(block, vd[...]).astype(BF16)
+        acc[at, :] = jnp.zeros((seq, acc.shape[1]), F32)
+
+    def add_plane(plane):
+        weights = W.at[pl.ds(pl.multiple_of(plane * plane_rows, plane_rows), plane_rows)]
+        columns = pl.ds(pl.multiple_of(plane * plane_rows, plane_rows), plane_rows)
+
+        @pl.loop(0, tiles)
+        def _(i):
+            at = pl.ds(pl.multiple_of(i * seq, seq), seq)
+            acc[at, :] += dot(N[at, columns], weights[...])
+
+    add_plane(z)
+    for t in range(chain - 1):
+        if t == chain - 2 and t > 0:
+            for half in range(2):
+                recv_chain(t, half)
+
+        @pl.when(z - 1 - t >= 0)
+        def _():
+            add_plane(z - 1 - t)
+
+        @pl.when(z + 1 + t <= chain - 1)
+        def _():
+            add_plane(z + 1 + t)
+
+    h = head_of(0)
+    qu_own = qu[:, pl.ds(pl.multiple_of(h * qcols, qcols), qcols)]
+    vu_own = vu[:, pl.ds(pl.multiple_of(h * kcols, kcols), kcols)]
+    local[4].wait()
+    local[5].wait()
+    for r in range(1, PLANE):
+        at = G.at[tok_rows(r)]
+        remote(at, at, g_send.at[r], g_recv.at[r], peer(r)).wait_recv()
+        at = SG.at[tok_rows(r)]
+        remote(at, at, s_send.at[r], s_recv.at[r], peer(r)).wait_recv()
+
+    pos_i = lax.broadcasted_iota(jnp.int32, (seq, seq), 0)
+    pos_j = lax.broadcasted_iota(jnp.int32, (seq, seq), 1)
+    band = (pos_j <= pos_i) & (pos_j > pos_i - 2 * tok)
+
+    @pl.loop(0, tiles)
+    def _(i):
+        at = pl.ds(pl.multiple_of(i * seq, seq), seq)
+        q_all = (acc[at, 0:qcols] + ADAPTER_NAME * dot(LQ[at, :], qu_own)).astype(BF16)
+        k = acc[at, qcols:qcols + kcols].astype(BF16)
+        v = (acc[at, qcols + kcols:] + ADAPTER_NAME * dot(LV[at, :], vu_own)).astype(BF16)
+        g_all = G[at, :]
+        own = SG[at, :].astype(F32)
+        across = jnp.concatenate([own] * (seq // own.shape[1]), axis=1)
+        along = jnp.concatenate([own[:tok].T, own[tok:].T], axis=1)[0:1, :]
+        mask = band & (across == along)
+        dv = jnp.zeros((seq, kcols), F32)
+        for n in range(qcols // kcols):
+            q = q_all[:, n * kcols:(n + 1) * kcols]
+            g = g_all[:, n * kcols:(n + 1) * kcols]
+            s = dot(q, k, ((1,), (1,))) * QSCALE
+            t = jnp.tanh(s / CAP)
+            expo = jnp.where(mask, jnp.exp(CAP * t), 0.0)
+            weights = expo / jnp.sum(expo, axis=-1, keepdims=True)
+            weights16 = weights.astype(BF16)
+            attended = dot(weights16, v)
+            dweight = dot(g, v, ((1,), (1,)))
+            delta = jnp.sum(g.astype(F32) * attended, axis=-1, keepdims=True)
+            dscore = (weights * (dweight - delta) * (1.0 - t * t) * QSCALE).astype(BF16)
+            DQ[at, n * kcols:(n + 1) * kcols] = dot(dscore, k).astype(BF16)
+            dv = dv + dot(weights16, g, ((0,), (0,)))
+        DV[at, :] = dv.astype(BF16)
+
+    pull_q = dot(qu_own, DQ[...], ((1,), (1,))).astype(BF16)
+    pull_v = dot(vu_own, DV[...], ((1,), (1,))).astype(BF16)
+    pull = jnp.concatenate([pull_q, pull_v], axis=0)
+    ranks = pull.shape[0]
+    half_rank = ranks // 2
+    r1_copies = []
+    for r in (7, 6, 5, 4, 3, 2, 1, 0):
+        columns = pl.ds(pl.multiple_of(head_of(r) * piece, piece), piece)
+        A[r] = dot(pull, N[:, columns])
+        if r > 0:
+            copy = remote(A.at[r], RA.at[r], r1_send.at[r], r1_recv.at[r], peer(r))
+            copy.start()
+            r1_copies.append(copy)
+    S[ranks:, 0:qcols] = dot(LQ[...], DQ[...], ((0,), (0,)))
+    S[ranks:, qcols:qcols + kcols] = dot(LV[...], DV[...], ((0,), (0,)))
+    for copy in r1_copies:
+        copy.wait_recv()
+    total = A[0]
+    for r in range(1, PLANE):
+        total = total + RA[r]
+    S[0:ranks, :] = total
+    r2_copies = []
+    for d in range(1, chain):
+        copy = remote(S, RS.at[d], r2_send.at[d], r2_recv.at[d], above((z + d) % chain))
+        copy.start()
+        r2_copies.append(copy)
+    for copy in r2_copies:
+        copy.wait_recv()
+    total = S[...]
+    for d in range(1, chain):
+        total = total + RS[d]
+    total = total * coefficient
+    T[...] = total
+    r3_copies = []
+    for r in (7, 6, 5, 4, 3, 2, 1):
+        copy = remote(T, OUT.at[r], r3_send.at[r], r3_recv.at[r], peer(r))
+        copy.start()
+        r3_copies.append(copy)
+
+    def put(r, value):
+        hp = head_of(r)
+        fcols = pl.ds(pl.multiple_of(hp * piece, piece), piece)
+        out_aq[:, fcols] = value[0:half_rank]
+        out_av[:, fcols] = value[half_rank:ranks]
+        out_bq[:, pl.ds(pl.multiple_of(hp * qcols, qcols), qcols)] = value[ranks:, 0:qcols]
+        out_bv[:, pl.ds(pl.multiple_of(hp * kcols, kcols), kcols)] = value[ranks:, qcols:qcols + kcols]
+
+    put(0, total)
+    for i, r in enumerate((7, 6, 5, 4, 3, 2, 1)):
+        r3_copies[i].wait_recv()
+    for r in range(1, PLANE):
+        put(r, OUT[r])
+
+    for r in (1, 2, 3):
+        for copy in w_copies[r]:
+            copy.wait_send()
+    for r in range(1, PLANE):
+        t_copies[r].wait_send()
+        g_copies[r].wait_send()
+        s_copies[r].wait_send()
+    for t in range(chain - 1):
+        for half in range(2):
+            @pl.when(has_up(t))
+            def _():
+                up_copy(t, half).wait_send()
+
+            @pl.when(has_down(t))
+            def _():
+                down_copy(t, half).wait_send()
+    for copy in r1_copies + r2_copies + r3_copies:
+        copy.wait_send()
+
+
+def on_plane(
+    tokens,
+    trace_index,
+    input_norm_scale,
+    query_weight,
+    key_weight,
+    value_weight,
+    query_down_weight,
+    query_up_weight,
+    value_down_weight,
+    value_up_weight,
+    output_gradient,
+):
+    tok = tokens.shape[1]
+    feats = tokens.shape[2]
+    fsdp = lax.axis_size("fsdp")
+    chain = fsdp // 4
+    ranks = query_down_weight.shape[1]
+    qcols = query_weight.shape[1] // PLANE
+    kcols = key_weight.shape[1] // PLANE
+    columns = qcols + 2 * kcols
+    piece = feats // PLANE
+    many = PLANE * tok
+    normed = normed_rows(tokens.reshape(tok, feats), input_norm_scale)
+    seg = jnp.broadcast_to(trace_index.reshape(tok, 1), (tok, 128)).astype(BF16)
+    token_total = lax.axis_size("ctx") * fsdp * tok
+    coefficient = ADAPTER_NAME / math.sqrt(token_total)
+    hbm = pl.BlockSpec(memory_space=pl.ANY)
+    vmem = pl.BlockSpec(memory_space=pltpu.VMEM)
+    dma = pltpu.SemaphoreType.DMA
+    steps = max(chain - 1, 1)
+    aq, bq, av, bv = pl.pallas_call(
+        functools.partial(plane_kernel, chain, coefficient),
+        out_shape=(
+            jax.ShapeDtypeStruct((ranks, feats), F32),
+            jax.ShapeDtypeStruct((ranks, query_weight.shape[1]), F32),
+            jax.ShapeDtypeStruct((ranks, feats), F32),
+            jax.ShapeDtypeStruct((ranks, value_weight.shape[1]), F32),
+        ),
+        in_specs=[hbm, hbm, hbm, hbm, hbm, vmem, vmem, vmem, vmem, hbm],
+        out_specs=(vmem, vmem, vmem, vmem),
+        scratch_shapes=[
+            pltpu.VMEM((many, feats), BF16),
+            pltpu.VMEM((feats, columns), BF16),
+            pltpu.VMEM((many, qcols), BF16),
+            pltpu.VMEM((many, 128), BF16),
+            pltpu.VMEM((many, columns), F32),
+            pltpu.VMEM((many, qcols), BF16),
+            pltpu.VMEM((many, kcols), BF16),
+            pltpu.VMEM((many, ranks), BF16),
+            pltpu.VMEM((many, ranks), BF16),
+            pltpu.VMEM((PLANE, 2 * ranks, piece), F32),
+            pltpu.VMEM((PLANE, 2 * ranks, piece), F32),
+            pltpu.VMEM((3 * ranks, piece), F32),
+            pltpu.VMEM((chain, 3 * ranks, piece), F32),
+            pltpu.VMEM((3 * ranks, piece), F32),
+            pltpu.VMEM((PLANE, 3 * ranks, piece), F32),
+            dma((6,)),
+            dma((4, 3)), dma((4, 3)),
+            dma((8,)), dma((8,)), dma((8,)), dma((8,)), dma((8,)), dma((8,)),
+            dma((steps, 2)), dma((steps, 2)), dma((steps, 2)), dma((steps, 2)),
+            dma((8,)), dma((8,)), dma((max(chain, 2),)), dma((max(chain, 2),)), dma((8,)), dma((8,)),
+        ],
+        compiler_params=pltpu.CompilerParams(
+            collective_id=0, has_side_effects=True, vmem_limit_bytes=56 * 1024 * 1024
+        ),
+    )(
+        normed, seg, query_weight, key_weight, value_weight,
+        query_down_weight, query_up_weight, value_down_weight, value_up_weight,
+        output_gradient.reshape(tok, output_gradient.shape[2]),
+    )
+    return (aq.T, bq, av.T, bv)
+
+
 def solution(mesh):
+    shape = mesh.shape
+    planes = shape["groups"] == 1 and shape["ctx"] == 2 and shape["fsdp"] % 4 == 0 and shape["fsdp"] > 8
     return jax.shard_map(
-        on_device,
+        on_plane if planes else on_device,
         mesh=mesh,
         in_specs=(
             P(("groups", "fsdp"), "ctx", None),

time: 446 us -> 107 us (0.24)
  waiting for transfers between devices: 344 us -> 0 us
  Pallas kernels: 0 us -> 95.3 us
  matrix products: 57 us -> 0 us
  starting transfers between devices: 13.8 us -> 0 us
  between operations: 14.1 us -> 0.69 us
  other arithmetic: 11.5 us -> 3.27 us
    all_gather x3 -> x0, waiting for transfers between devices: 202 us -> none  [the longest x1 85.4 us: on_device(): lax.all_gather(query_weight, 'fsdp', axis=0, tiled=True)]
    psum x1 -> x0, waiting for transfers between devices: 127 us -> none  [on_device(): lax.psum((part_aq, part_bq, part_av, part_bv), ('ctx', 'fsdp'))]
    pallas_call x0 -> x1, Pallas kernels: none -> 95.3 us  [on_plane(): pl.pallas_call(functools.partial(plane_kernel, chain, coefficient), out_s...]
    dot_general x44 -> x0, matrix products: 57 us -> none  [the longest x8 15.3 us: attend_head(): jnp.einsum('gij,jd->igd', dscore, k_head, preferred_element_type=jnp.floa...]
    ppermute x8 -> x0, starting transfers between devices: 13.6 us -> none  [shifted(): return lax.ppermute(value, axis, pairs)]
    ppermute x8 -> x0, waiting for transfers between devices: 13.2 us -> none  [shifted(): return lax.ppermute(value, axis, pairs)]
    unnamed x39 -> x18, local copies, waits for them, and re-layouts: 0.35 us -> 6.91 us
    mul x3 -> x0, other arithmetic: 4.83 us -> none  [the longest x1 1.79 us: on_device(): sum_av * coefficient]
  transfers between devices with their start and end apart: 12 -> 0, of which waited for: 6 -> 0; matrix products, arithmetic and copies ran while one was open for 4% -> 0% of each run, Pallas kernels for 0% -> 0%
where the time goes in v1:
time: 107 us
  Pallas kernels  95.3 us (89%)
  local copies, waits for them, and re-layouts  7.61 us (7%)
  other arithmetic  3.27 us (3%)
    pallas_call x1, Pallas kernels, on_plane(): pl.pallas_call(functools.partial(plane_kernel, chain, coefficient), out_s...  95.3 us
    unnamed x18, local copies, waits for them, and re-layouts  6.91 us

profile of v1, /device:TPU:0, one launch (start us, length us, event | category | flops | bytes accessed | tf_op | source)
XLA Modules:
  0.0 106.9 jit_solution(10337931935835363409)
XLA Ops:
  0.6 0.0 copy-start
  0.6 0.0 copy-start.5
  0.7 0.7 convert_bitcast_fusion
  1.4 1.4 %fusion = f32[128]{0:T(128)S(1)} fusion(bf16[1,128,3072]{2,1,0:T(8,128)(2,1)} %param.11), kind=kLoop, calls=%fused_computation.2 | loop fusion | flops 1179520 | bytes 786944 | tf_op jit(solution)/shard_map/reduce_sum | solution.py:28
  2.8 0.0 copy-done.5
  2.8 0.7 broadcast_in_dim.2.seg
  3.5 0.0 copy-done
  3.5 0.0 copy-start.2
  3.5 1.2 %fusion.2.norm = bf16[128,3072]{1,0:T(8,128)(2,1)} fusion(bf16[1,128,3072]{2,1,0:T(8,128)(2,1)S(1)} %copy-done, f32[3072]{0:T(1024)S(1)} %convert_element_type.19, f32[128]{0:T(128)S(1)} %add_rsqrt_fusion), kind=kLoop, calls=%fused_computation.4 | loop fusion | flops 1572864 | bytes 1585664 | tf_op jit(solution)/shard_map/convert_element_type | solution.py:29
  4.6 0.0 copy-done.2
  4.7 0.0 copy-start.3
  4.7 1.2 %copy.15.qd = bf16[3072,16]{1,0:T(8,128)(2,1)} copy(bf16[3072,16]{0,1:T(8,128)(2,1)S(1)} %copy-done.2) | data formatting | bytes 196608 | tf_op args[6]
  5.8 0.0 copy-done.3
  5.8 1.2 %copy.16.vd = bf16[3072,16]{1,0:T(8,128)(2,1)} copy(bf16[3072,16]{0,1:T(8,128)(2,1)S(1)} %copy-done.3) | data formatting | bytes 196608 | tf_op args[8]
  7.0 95.3 %shard_map.138 = (f32[16,3072]{1,0:T(8,128)}, f32[16,2048]{1,0:T(8,128)}, f32[16,3072]{1,0:T(8,128)}, f32[16,1024]{1,0:T(8,128)}) custom-call(bf16[128,3072]{1,0:T(8,128)(2,1)} %fusion.2.norm, bf16[128,128]{1,0:T(8,128)(2,1)} %broadcast_in_dim.2.seg, bf16[192,2048]{1,0:T(8,128)(2,1)} %wq.1, bf16[192,1024]{1,0:T(8,128)(2,1)} %wk.1, bf16[192,1024]{1,0:T(8,128)(2,1)} %wv.1, ...), custom_call_target="tpu_custom_call" | custom-call | tf_op jit(solution)/shard_map/pallas_call | solution.py:545
  102.3 0.0 copy-start.1
  102.3 0.0 copy-start.4
  102.4 1.7 %copy.21 = f32[3072,16]{0,1:T(8,128)} copy(f32[3072,16]{0,1:T(8,128)} %bitcast.11) | data formatting | bytes 393216
  104.0 1.6 %copy.22 = f32[16,2048]{1,0:T(8,128)} copy(f32[16,2048]{1,0:T(8,128)} %get-tuple-element.17) | data formatting | bytes 262144
  105.6 0.0 copy-done.1
  105.6 0.7 copy.23
  106.3 0.0 copy-done.4
  106.3 0.6 copy.24
  (2 shorter events, 0.0 us)
Async XLA Ops:
  0.6 2.9 %copy-start = (bf16[1,128,3072]{2,1,0:T(8,128)(2,1)S(1)}, bf16[1,128,3072]{2,1,0:T(8,128)(2,1)}, u32[]{:S(2)}) copy-start(bf16[1,128,3072]{2,1,0:T(8,128)(2,1)} %param.11) | copy-start | bytes 2359300
  0.6 2.1 %copy-start.5 = (bf16[3072]{0:T(1024)(128)(2,1)S(1)}, bf16[3072]{0:T(1024)(128)(2,1)}, u32[]{:S(2)}) copy-start(bf16[3072]{0:T(1024)(128)(2,1)} %param.13) | copy-start | bytes 18436
  3.5 1.2 %copy-start.2 = (bf16[3072,16]{0,1:T(8,128)(2,1)S(1)}, bf16[3072,16]{0,1:T(8,128)(2,1)}, u32[]{:S(2)}) copy-start(bf16[3072,16]{0,1:T(8,128)(2,1)} %param.17) | copy-start | bytes 294916
  4.7 1.2 %copy-start.3 = (bf16[3072,16]{0,1:T(8,128)(2,1)S(1)}, bf16[3072,16]{0,1:T(8,128)(2,1)}, u32[]{:S(2)}) copy-start(bf16[3072,16]{0,1:T(8,128)(2,1)} %param.19) | copy-start | bytes 294916
  102.3 3.2 %copy-start.1 = (f32[16,3072]{1,0:T(8,128)S(1)}, f32[16,3072]{1,0:T(8,128)}, u32[]{:S(2)}) copy-start(f32[16,3072]{1,0:T(8,128)} %get-tuple-element.10) | copy-start | bytes 589828
  102.3 3.9 %copy-start.4 = (f32[16,1024]{1,0:T(8,128)S(1)}, f32[16,1024]{1,0:T(8,128)}, u32[]{:S(2)}) copy-start(f32[16,1024]{1,0:T(8,128)} %get-tuple-element.19) | copy-start | bytes 196612

commit v2 on v1

--- a/solution.py
+++ b/solution.py
@@ -176,9 +176,9 @@
 
 def plane_kernel(
     chain, coefficient,
-    norm, seg, wq, wk, wv, qd, qu, vd, vu, grad,
-    out_aq, out_bq, out_av, out_bv,
-    N, W, G, SG, acc, DQ, DV, LQ, LV, A, RA, S, RS, T, OUT,
+    raw, seg, gain, wq, wk, wv, qd, qu, vd, vu, grad,
+    OUT,
+    N, M, W, G, SG, acc, DQ, DV, LQ, LV, A, RA, RS, T,
     local_sem, w_send, w_recv, t_send, t_recv, g_send, g_recv, s_send, s_recv,
     up_send, up_recv, down_send, down_recv,
     r1_send, r1_recv, r2_send, r2_recv, r3_send, r3_recv,
@@ -188,7 +188,7 @@
     z = f // 4
     y = (f // 2) % 2
     c = f % 2
-    tok, feats = norm.shape
+    tok, feats = raw.shape
     rows = wq.shape[0]
     qcols = wq.shape[1] // PLANE
     kcols = wk.shape[1] // PLANE
@@ -216,6 +216,17 @@
     def tok_rows(r):
         px, py, pc = coords(r)
         return pl.ds(pl.multiple_of(((py * 2 + pc) * 2 + px) * tok, tok), tok)
+
+    def tok_slot(r):
+        px, py, pc = coords(r)
+        return (py * 2 + pc) * 2 + px
+
+    def tok_piece(r, part):
+        px, py, pc = coords(r)
+        if part is None:
+            return tok_rows(r)
+        begin = ((py * 2 + pc) * 2 + px) * tok + part * (tok // 2)
+        return pl.ds(pl.multiple_of(begin, tok // 2), tok // 2)
 
     def remote(src, dst, send, recv, device):
         return pltpu.make_async_remote_copy(
@@ -249,9 +260,9 @@
         return grad.at[:, pl.ds(pl.multiple_of(h * qcols, qcols), qcols)]
 
     local = [pltpu.make_async_copy(a, b, local_sem.at[i]) for i, (a, b) in enumerate(w_parts(0))]
-    local.append(pltpu.make_async_copy(norm, N.at[tok_rows(0)], local_sem.at[3]))
+    local.append(pltpu.make_async_copy(raw, N.at[tok_rows(0)], local_sem.at[3]))
     local.append(pltpu.make_async_copy(g_cols(0), G.at[tok_rows(0)], local_sem.at[4]))
-    local.append(pltpu.make_async_copy(seg, SG.at[tok_rows(0)], local_sem.at[5]))
+    local.append(pltpu.make_async_copy(seg, SG.at[tok_slot(0)], local_sem.at[5]))
     for copy in local:
         copy.start()
     pl.semaphore_wait(barrier, PLANE - 1 + chain - 1)
@@ -263,15 +274,27 @@
         ]
         for copy in w_copies[r]:
             copy.start()
-    t_copies = {}
-    for r in (2, 4, 1):
-        t_copies[r] = remote(norm, N.at[tok_rows(0)], t_send.at[r], t_recv.at[r], peer(r))
-        t_copies[r].start()
+    t_copies = []
+
+    def send_token(r_mine, r_there, hop, part=None):
+        at = N.at[tok_piece(r_mine, part)]
+        source = at
+        if r_mine == 0:
+            source = raw if part is None else raw.at[pl.ds(part * (tok // 2), tok // 2)]
+        i = part or 0
+        copy = remote(source, at, t_send.at[r_there, i], t_recv.at[r_there, i], peer(hop))
+        copy.start()
+        t_copies.append(copy)
+
+    send_token(0, 2, 2, 0)
+    send_token(0, 2, 2, 1)
+    send_token(0, 4, 4)
+    send_token(0, 1, 1)
     g_copies = {}
     s_copies = {}
     for r in range(1, PLANE):
         g_copies[r] = remote(g_cols(r), G.at[tok_rows(0)], g_send.at[r], g_recv.at[r], peer(r))
-        s_copies[r] = remote(seg, SG.at[tok_rows(0)], s_send.at[r], s_recv.at[r], peer(r))
+        s_copies[r] = remote(seg, SG.at[tok_slot(0)], s_send.at[r], s_recv.at[r], peer(r))
 
     def half_rows(plane, half):
         py = y if half == 0 else 1 - y
@@ -317,20 +340,57 @@
         def _():
             down_arrival(t, half).wait_recv()
 
-    def forward_token(r_mine, r_there, hop):
-        at = N.at[tok_rows(r_mine)]
-        t_copies[r_there] = remote(at, at, t_send.at[r_there], t_recv.at[r_there], peer(hop))
-        t_copies[r_there].start()
-
-    def wait_token(r):
-        at = N.at[tok_rows(r)]
-        remote(at, at, t_send.at[r], t_recv.at[r], peer(1)).wait_recv()
+    def wait_token(r, part=None):
+        at = N.at[tok_piece(r, part)]
+        i = part or 0
+        remote(at, at, t_send.at[r, i], t_recv.at[r, i], peer(1)).wait_recv()
 
     def wait_weight(r):
         at = w_rows(r)
         for i, (lo, width) in enumerate(((0, qcols), (qcols, kcols), (qcols + kcols, kcols))):
             ref = W.at[at, pl.ds(lo, width)]
             remote(ref, ref, w_send.at[r, i], w_recv.at[r, i], peer(r)).wait_recv()
+
+    part_rows = 4 * tok
+
+    def part_at(part, i, height):
+        py = y if part == 0 else 1 - y
+        return pl.ds(pl.multiple_of(py * part_rows + i * height, height), height)
+
+    def prepare(part):
+        height = tok // 2
+
+        @pl.loop(0, part_rows // height)
+        def _(i):
+            at = part_at(part, i, height)
+            flt = N[at, :].astype(F32)
+            meansq = jnp.sum(flt * flt, axis=-1, keepdims=True) / feats
+            M[at, :] = (flt * lax.rsqrt(meansq + EPS) * gain[...].astype(F32)).astype(BF16)
+
+        @pl.loop(0, part_rows // seq)
+        def _(i):
+            at = part_at(part, i, seq)
+            block = M[at, :]
+            LQ[at, :] = dot(block, qd[...], ((1,), (1,))).astype(BF16)
+            LV[at, :] = dot(block, vd[...], ((1,), (1,))).astype(BF16)
+
+    def add_piece(plane, half, part, first=False):
+        chosen = half_rows(plane, half)
+
+        @pl.loop(0, part_rows // seq)
+        def _(i):
+            at = part_at(part, i, seq)
+            value = dot(M[at, chosen], W[chosen, :])
+            acc[at, :] = value if first else acc[at, :] + value
+
+    def add_step(t, half, part):
+        @pl.when(z - 1 - t >= 0)
+        def _():
+            add_piece(z - 1 - t, half, part)
+
+        @pl.when(z + 1 + t <= chain - 1)
+        def _():
+            add_piece(z + 1 + t, half, part)
 
     for i in range(3):
         local[i].wait()
@@ -340,61 +400,50 @@
     wait_weight(3)
     send_chain(0, 1)
     for r in range(1, PLANE):
+        s_copies[r].start()
+    recv_chain(0, 0)
+    send_chain(1, 0)
+    wait_token(4)
+    send_token(4, 5, 1)
+    wait_token(2, 0)
+    send_token(2, 6, 4, 0)
+    recv_chain(0, 1)
+    send_chain(1, 1)
+    local[3].wait()
+    wait_token(1)
+    wait_token(5)
+    prepare(0)
+    wait_token(2, 1)
+    send_token(2, 6, 4, 1)
+    send_token(2, 3, 1)
+    for r in range(1, PLANE):
         g_copies[r].start()
-        s_copies[r].start()
-    wait_token(4)
-    forward_token(4, 5, 1)
-    if chain > 1:
-        for half in range(2):
-            recv_chain(0, half)
-            if chain > 2:
-                send_chain(1, half)
-    wait_token(2)
-    forward_token(2, 6, 4)
-    forward_token(2, 3, 1)
+    add_piece(z, 0, 0, True)
+    add_piece(z, 1, 0)
+    for half in range(2):
+        add_step(0, half, 0)
     for t in range(1, chain - 2):
         for half in range(2):
             recv_chain(t, half)
             send_chain(t + 1, half)
-    wait_token(6)
-    forward_token(6, 7, 1)
-    local[3].wait()
-    for r in (1, 5, 3, 7):
-        wait_token(r)
+            add_step(t, half, 0)
+    wait_token(6, 0)
+    wait_token(6, 1)
+    send_token(6, 7, 1)
+    wait_token(3)
+    wait_token(7)
+    prepare(1)
+    add_piece(z, 0, 1, True)
+    add_piece(z, 1, 1)
+    for t in range(chain - 2):
+        for half in range(2):
+            add_step(t, half, 1)
+    for half in range(2):
+        recv_chain(chain - 2, half)
+        for part in range(2):
+            add_step(chain - 2, half, part)
 
     tiles = PLANE * tok // seq
-
-    @pl.loop(0, tiles)
-    def _(i):
-        at = pl.ds(pl.multiple_of(i * seq, seq), seq)
-        block = N[at, :]
-        LQ[at, :] = dot(block, qd[...]).astype(BF16)
-        LV[at, :] = dot(block, vd[...]).astype(BF16)
-        acc[at, :] = jnp.zeros((seq, acc.shape[1]), F32)
-
-    def add_plane(plane):
-        weights = W.at[pl.ds(pl.multiple_of(plane * plane_rows, plane_rows), plane_rows)]
-        columns = pl.ds(pl.multiple_of(plane * plane_rows, plane_rows), plane_rows)
-
-        @pl.loop(0, tiles)
-        def _(i):
-            at = pl.ds(pl.multiple_of(i * seq, seq), seq)
-            acc[at, :] += dot(N[at, columns], weights[...])
-
-    add_plane(z)
-    for t in range(chain - 1):
-        if t == chain - 2 and t > 0:
-            for half in range(2):
-                recv_chain(t, half)
-
-        @pl.when(z - 1 - t >= 0)
-        def _():
-            add_plane(z - 1 - t)
-
-        @pl.when(z + 1 + t <= chain - 1)
-        def _():
-            add_plane(z + 1 + t)
-
     h = head_of(0)
     qu_own = qu[:, pl.ds(pl.multiple_of(h * qcols, qcols), qcols)]
     vu_own = vu[:, pl.ds(pl.multiple_of(h * kcols, kcols), kcols)]
@@ -403,7 +452,7 @@
     for r in range(1, PLANE):
         at = G.at[tok_rows(r)]
         remote(at, at, g_send.at[r], g_recv.at[r], peer(r)).wait_recv()
-        at = SG.at[tok_rows(r)]
+        at = SG.at[tok_slot(r)]
         remote(at, at, s_send.at[r], s_recv.at[r], peer(r)).wait_recv()
 
     pos_i = lax.broadcasted_iota(jnp.int32, (seq, seq), 0)
@@ -417,9 +466,10 @@
         k = acc[at, qcols:qcols + kcols].astype(BF16)
         v = (acc[at, qcols + kcols:] + ADAPTER_NAME * dot(LV[at, :], vu_own)).astype(BF16)
         g_all = G[at, :]
-        own = SG[at, :].astype(F32)
-        across = jnp.concatenate([own] * (seq // own.shape[1]), axis=1)
-        along = jnp.concatenate([own[:tok].T, own[tok:].T], axis=1)[0:1, :]
+        traces = [SG[2 * i].astype(F32), SG[2 * i + 1].astype(F32)]
+        along = jnp.concatenate(traces, axis=1)
+        turned = [jnp.broadcast_to(own, (tok, tok)).T for own in traces]
+        across = jnp.concatenate([jnp.concatenate([own, own], axis=1) for own in turned], axis=0)
         mask = band & (across == along)
         dv = jnp.zeros((seq, kcols), F32)
         for n in range(qcols // kcols):
@@ -446,56 +496,49 @@
     r1_copies = []
     for r in (7, 6, 5, 4, 3, 2, 1, 0):
         columns = pl.ds(pl.multiple_of(head_of(r) * piece, piece), piece)
-        A[r] = dot(pull, N[:, columns])
+        A[r] = dot(pull, M[:, columns]).astype(BF16)
         if r > 0:
             copy = remote(A.at[r], RA.at[r], r1_send.at[r], r1_recv.at[r], peer(r))
             copy.start()
             r1_copies.append(copy)
-    S[ranks:, 0:qcols] = dot(LQ[...], DQ[...], ((0,), (0,)))
-    S[ranks:, qcols:qcols + kcols] = dot(LV[...], DV[...], ((0,), (0,)))
+    own_sum = RS.at[z]
+    own_sum[ranks:, 0:qcols] = dot(LQ[...], DQ[...], ((0,), (0,))).astype(BF16)
+    own_sum[ranks:, qcols:qcols + kcols] = dot(LV[...], DV[...], ((0,), (0,))).astype(BF16)
     for copy in r1_copies:
         copy.wait_recv()
-    total = A[0]
-    for r in range(1, PLANE):
-        total = total + RA[r]
-    S[0:ranks, :] = total
+    total = A[0].astype(F32)
+    for r in range(1, PLANE):
+        total = total + RA[r].astype(F32)
+    own_sum[0:ranks, :] = total.astype(BF16)
     r2_copies = []
     for d in range(1, chain):
-        copy = remote(S, RS.at[d], r2_send.at[d], r2_recv.at[d], above((z + d) % chain))
+        copy = remote(own_sum, own_sum, r2_send.at[d], r2_recv.at[d], above((z + d) % chain))
         copy.start()
         r2_copies.append(copy)
-    for copy in r2_copies:
-        copy.wait_recv()
-    total = S[...]
     for d in range(1, chain):
-        total = total + RS[d]
-    total = total * coefficient
+        at = RS.at[(z - d + chain) % chain]
+        remote(at, at, r2_send.at[d], r2_recv.at[d], above((z + d) % chain)).wait_recv()
+    total = RS[0].astype(F32)
+    for d in range(1, chain):
+        total = total + RS[d].astype(F32)
+    total = (total * coefficient).astype(BF16)
     T[...] = total
     r3_copies = []
     for r in (7, 6, 5, 4, 3, 2, 1):
-        copy = remote(T, OUT.at[r], r3_send.at[r], r3_recv.at[r], peer(r))
+        copy = remote(T, OUT.at[h], r3_send.at[r], r3_recv.at[r], peer(r))
         copy.start()
         r3_copies.append(copy)
-
-    def put(r, value):
-        hp = head_of(r)
-        fcols = pl.ds(pl.multiple_of(hp * piece, piece), piece)
-        out_aq[:, fcols] = value[0:half_rank]
-        out_av[:, fcols] = value[half_rank:ranks]
-        out_bq[:, pl.ds(pl.multiple_of(hp * qcols, qcols), qcols)] = value[ranks:, 0:qcols]
-        out_bv[:, pl.ds(pl.multiple_of(hp * kcols, kcols), kcols)] = value[ranks:, qcols:qcols + kcols]
-
-    put(0, total)
-    for i, r in enumerate((7, 6, 5, 4, 3, 2, 1)):
-        r3_copies[i].wait_recv()
-    for r in range(1, PLANE):
-        put(r, OUT[r])
+    OUT[h] = total
+    for r in range(1, PLANE):
+        at = OUT.at[head_of(r)]
+        remote(at, at, r3_send.at[r], r3_recv.at[r], peer(r)).wait_recv()
 
     for r in (1, 2, 3):
         for copy in w_copies[r]:
             copy.wait_send()
-    for r in range(1, PLANE):
-        t_copies[r].wait_send()
+    for copy in t_copies:
+        copy.wait_send()
+    for r in range(1, PLANE):
         g_copies[r].wait_send()
         s_copies[r].wait_send()
     for t in range(chain - 1):
@@ -509,6 +552,19 @@
                 down_copy(t, half).wait_send()
     for copy in r1_copies + r2_copies + r3_copies:
         copy.wait_send()
+
+
+def unpack_kernel(gathered, out_aq, out_bq, out_av, out_bv):
+    ranks, feats = out_aq.shape
+    piece = feats // PLANE
+    qcols = out_bq.shape[1] // PLANE
+    kcols = out_bv.shape[1] // PLANE
+    for h in range(PLANE):
+        value = gathered[h].astype(F32)
+        out_aq[:, h * piece:(h + 1) * piece] = value[0:ranks]
+        out_av[:, h * piece:(h + 1) * piece] = value[ranks:2 * ranks]
+        out_bq[:, h * qcols:(h + 1) * qcols] = value[2 * ranks:, 0:qcols]
+        out_bv[:, h * kcols:(h + 1) * kcols] = value[2 * ranks:, qcols:qcols + kcols]
 
 
 def on_plane(
@@ -534,43 +590,35 @@
     columns = qcols + 2 * kcols
     piece = feats // PLANE
     many = PLANE * tok
-    normed = normed_rows(tokens.reshape(tok, feats), input_norm_scale)
-    seg = jnp.broadcast_to(trace_index.reshape(tok, 1), (tok, 128)).astype(BF16)
     token_total = lax.axis_size("ctx") * fsdp * tok
     coefficient = ADAPTER_NAME / math.sqrt(token_total)
     hbm = pl.BlockSpec(memory_space=pl.ANY)
     vmem = pl.BlockSpec(memory_space=pltpu.VMEM)
     dma = pltpu.SemaphoreType.DMA
     steps = max(chain - 1, 1)
-    aq, bq, av, bv = pl.pallas_call(
+    gathered = pl.pallas_call(
         functools.partial(plane_kernel, chain, coefficient),
-        out_shape=(
-            jax.ShapeDtypeStruct((ranks, feats), F32),
-            jax.ShapeDtypeStruct((ranks, query_weight.shape[1]), F32),
-            jax.ShapeDtypeStruct((ranks, feats), F32),
-            jax.ShapeDtypeStruct((ranks, value_weight.shape[1]), F32),
-        ),
-        in_specs=[hbm, hbm, hbm, hbm, hbm, vmem, vmem, vmem, vmem, hbm],
-        out_specs=(vmem, vmem, vmem, vmem),
+        out_shape=jax.ShapeDtypeStruct((PLANE, 3 * ranks, piece), BF16),
+        in_specs=[hbm, hbm, vmem, hbm, hbm, hbm, vmem, vmem, vmem, vmem, hbm],
+        out_specs=vmem,
         scratch_shapes=[
+            pltpu.VMEM((many, feats), BF16),
             pltpu.VMEM((many, feats), BF16),
             pltpu.VMEM((feats, columns), BF16),
             pltpu.VMEM((many, qcols), BF16),
-            pltpu.VMEM((many, 128), BF16),
+            pltpu.VMEM((PLANE, 1, tok), jnp.int32),
             pltpu.VMEM((many, columns), F32),
             pltpu.VMEM((many, qcols), BF16),
             pltpu.VMEM((many, kcols), BF16),
             pltpu.VMEM((many, ranks), BF16),
             pltpu.VMEM((many, ranks), BF16),
-            pltpu.VMEM((PLANE, 2 * ranks, piece), F32),
-            pltpu.VMEM((PLANE, 2 * ranks, piece), F32),
-            pltpu.VMEM((3 * ranks, piece), F32),
-            pltpu.VMEM((chain, 3 * ranks, piece), F32),
-            pltpu.VMEM((3 * ranks, piece), F32),
-            pltpu.VMEM((PLANE, 3 * ranks, piece), F32),
+            pltpu.VMEM((PLANE, 2 * ranks, piece), BF16),
+            pltpu.VMEM((PLANE, 2 * ranks, piece), BF16),
+            pltpu.VMEM((chain, 3 * ranks, piece), BF16),
+            pltpu.VMEM((3 * ranks, piece), BF16),
             dma((6,)),
             dma((4, 3)), dma((4, 3)),
-            dma((8,)), dma((8,)), dma((8,)), dma((8,)), dma((8,)), dma((8,)),
+            dma((8, 2)), dma((8, 2)), dma((8,)), dma((8,)), dma((8,)), dma((8,)),
             dma((steps, 2)), dma((steps, 2)), dma((steps, 2)), dma((steps, 2)),
             dma((8,)), dma((8,)), dma((max(chain, 2),)), dma((max(chain, 2),)), dma((8,)), dma((8,)),
         ],
@@ -578,10 +626,22 @@
             collective_id=0, has_side_effects=True, vmem_limit_bytes=56 * 1024 * 1024
         ),
     )(
-        normed, seg, query_weight, key_weight, value_weight,
-        query_down_weight, query_up_weight, value_down_weight, value_up_weight,
+        tokens.reshape(tok, feats), trace_index, input_norm_scale.reshape(1, feats),
+        query_weight, key_weight, value_weight,
+        query_down_weight.T, query_up_weight, value_down_weight.T, value_up_weight,
         output_gradient.reshape(tok, output_gradient.shape[2]),
     )
+    aq, bq, av, bv = pl.pallas_call(
+        unpack_kernel,
+        out_shape=(
+            jax.ShapeDtypeStruct((ranks, feats), F32),
+            jax.ShapeDtypeStruct((ranks, query_weight.shape[1]), F32),
+            jax.ShapeDtypeStruct((ranks, feats), F32),
+            jax.ShapeDtypeStruct((ranks, value_weight.shape[1]), F32),
+        ),
+        in_specs=[vmem],
+        out_specs=(vmem, vmem, vmem, vmem),
+    )(gathered)
     return (aq.T, bq, av.T, bv)
 
 

time: 107 us -> 86.1 us (0.80)
  Pallas kernels: 95.3 us -> 84 us
  local copies, waits for them, and re-layouts: 7.61 us -> 1.29 us
  other arithmetic: 3.27 us -> 0 us
    pallas_call x1, Pallas kernels: 95.3 us -> 82.2 us  [on_plane(): pl.pallas_call(functools.partial(plane_kernel, chain, coefficient), out_s...]
    unnamed x18 -> x2, local copies, waits for them, and re-layouts: 6.91 us -> 0.68 us
    convert_element_type x3 -> x0, other arithmetic: 1.89 us -> none  [the longest x1 1.15 us: normed_rows(): (flt * lax.rsqrt(meansq + EPS) * gain.astype(jnp.float32)).astype(jnp.bfl...]
    pallas_call x0 -> x1, Pallas kernels: none -> 1.78 us  [on_plane(): pl.pallas_call(unpack_kernel, out_shape=(jax.ShapeDtypeStruct((ranks, fea...]
    reduce_sum x1 -> x0, other arithmetic: 1.37 us -> none  [normed_rows(): meansq = jnp.mean(flt * flt, axis=-1, keepdims=True)]
where the time goes in v2:
time: 86.1 us; the launch traced here: 85.9 us
  Pallas kernels  84 us (98%)
  local copies, waits for them, and re-layouts  1.29 us (1%)
    pallas_call x1, Pallas kernels, on_plane(): pl.pallas_call(functools.partial(plane_kernel, chain, coefficient), out_s...  82.2 us
    pallas_call x1, Pallas kernels, on_plane(): pl.pallas_call(unpack_kernel, out_shape=(jax.ShapeDtypeStruct((ranks, fea...  1.78 us

profile of v2, /device:TPU:0, one launch (start us, length us, event | category | flops | bytes accessed | tf_op | source)
XLA Modules:
  0.0 85.9 jit_solution(13653205899022927937)
XLA Ops:
  0.6 0.0 copy-start
  0.6 0.7 copy-done
  1.3 0.6 reshape.18.gain
  1.9 82.2 %shard_map.138.gathered = bf16[8,48,384]{2,1,0:T(8,128)(2,1)} custom-call(bf16[128,3072]{1,0:T(8,128)(2,1)} %bitcast.6, s32[1,128]{1,0:T(1,128)} %seg.1, bf16[1,3072]{1,0:T(2,128)(2,1)} %reshape.18.gain, bf16[192,2048]{1,0:T(8,128)(2,1)} %wq.1, bf16[192,1024]{1,0:T(8,128)(2,1)} %wk.1, bf16[192,1024]{1,0:T(8,128)(2,1)} %wv.1, bf16[16,3072]{1,0:T(8,128)(2,1)} %bitcast.8, ...), custom_call_target="tpu_custom_call" | custom-call | tf_op jit(solution)/shard_map/pallas_call | solution.py:599
  84.2 1.8 %shard_map.139 = (f32[16,3072]{1,0:T(8,128)}, f32[16,2048]{1,0:T(8,128)}, f32[16,3072]{1,0:T(8,128)}, f32[16,1024]{1,0:T(8,128)}) custom-call(bf16[8,48,384]{2,1,0:T(8,128)(2,1)} %shard_map.138.gathered), custom_call_target="tpu_custom_call" | custom-call | tf_op jit(solution)/shard_map/pallas_call | solution.py:634
Async XLA Ops:
  0.6 0.7 copy-start

commit v3 on v2

--- a/solution.py
+++ b/solution.py
@@ -357,22 +357,22 @@
         py = y if part == 0 else 1 - y
         return pl.ds(pl.multiple_of(py * part_rows + i * height, height), height)
 
-    def prepare(part):
+    def prepare(r):
         height = tok // 2
 
-        @pl.loop(0, part_rows // height)
+        @pl.loop(0, 2)
         def _(i):
-            at = part_at(part, i, height)
+            px, py, pc = coords(r)
+            begin = ((py * 2 + pc) * 2 + px) * tok + i * height
+            at = pl.ds(pl.multiple_of(begin, height), height)
             flt = N[at, :].astype(F32)
             meansq = jnp.sum(flt * flt, axis=-1, keepdims=True) / feats
-            M[at, :] = (flt * lax.rsqrt(meansq + EPS) * gain[...].astype(F32)).astype(BF16)
-
-        @pl.loop(0, part_rows // seq)
-        def _(i):
-            at = part_at(part, i, seq)
-            block = M[at, :]
-            LQ[at, :] = dot(block, qd[...], ((1,), (1,))).astype(BF16)
-            LV[at, :] = dot(block, vd[...], ((1,), (1,))).astype(BF16)
+            M[at, :] = (flt * lax.rsqrt(meansq + EPS) * gain[...].astype(F32).reshape(1, feats)).astype(BF16)
+
+        at = tok_rows(r)
+        block = M[at, :]
+        LQ[at, :] = dot(block, qd[...], ((1,), (1,))).astype(BF16)
+        LV[at, :] = dot(block, vd[...], ((1,), (1,))).astype(BF16)
 
     def add_piece(plane, half, part, first=False):
         chosen = half_rows(plane, half)
@@ -403,25 +403,31 @@
         s_copies[r].start()
     recv_chain(0, 0)
     send_chain(1, 0)
+    local[3].wait()
+    prepare(0)
+    wait_token(1)
+    prepare(1)
     wait_token(4)
     send_token(4, 5, 1)
     wait_token(2, 0)
     send_token(2, 6, 4, 0)
     recv_chain(0, 1)
     send_chain(1, 1)
-    local[3].wait()
-    wait_token(1)
+    prepare(4)
     wait_token(5)
-    prepare(0)
+    prepare(5)
     wait_token(2, 1)
     send_token(2, 6, 4, 1)
     send_token(2, 3, 1)
     for r in range(1, PLANE):
         g_copies[r].start()
+    prepare(2)
     add_piece(z, 0, 0, True)
     add_piece(z, 1, 0)
     for half in range(2):
         add_step(0, half, 0)
+    wait_token(3)
+    prepare(3)
     for t in range(1, chain - 2):
         for half in range(2):
             recv_chain(t, half)
@@ -430,9 +436,9 @@
     wait_token(6, 0)
     wait_token(6, 1)
     send_token(6, 7, 1)
-    wait_token(3)
+    prepare(6)
     wait_token(7)
-    prepare(1)
+    prepare(7)
     add_piece(z, 0, 1, True)
     add_piece(z, 1, 1)
     for t in range(chain - 2):
@@ -459,7 +465,7 @@
     pos_j = lax.broadcasted_iota(jnp.int32, (seq, seq), 1)
     band = (pos_j <= pos_i) & (pos_j > pos_i - 2 * tok)
 
-    @pl.loop(0, tiles)
+    @pl.loop(0, tiles, unroll=2)
     def _(i):
         at = pl.ds(pl.multiple_of(i * seq, seq), seq)
         q_all = (acc[at, 0:qcols] + ADAPTER_NAME * dot(LQ[at, :], qu_own)).astype(BF16)
@@ -475,16 +481,15 @@
         for n in range(qcols // kcols):
             q = q_all[:, n * kcols:(n + 1) * kcols]
             g = g_all[:, n * kcols:(n + 1) * kcols]
-            s = dot(q, k, ((1,), (1,))) * QSCALE
-            t = jnp.tanh(s / CAP)
+            t = jnp.tanh(dot(q, k, ((1,), (1,))) * (QSCALE / CAP))
             expo = jnp.where(mask, jnp.exp(CAP * t), 0.0)
-            weights = expo / jnp.sum(expo, axis=-1, keepdims=True)
+            weights = expo * (1.0 / jnp.sum(expo, axis=-1, keepdims=True))
             weights16 = weights.astype(BF16)
             attended = dot(weights16, v)
             dweight = dot(g, v, ((1,), (1,)))
             delta = jnp.sum(g.astype(F32) * attended, axis=-1, keepdims=True)
-            dscore = (weights * (dweight - delta) * (1.0 - t * t) * QSCALE).astype(BF16)
-            DQ[at, n * kcols:(n + 1) * kcols] = dot(dscore, k).astype(BF16)
+            dscore = (weights * (dweight - delta) * (1.0 - t * t)).astype(BF16)
+            DQ[at, n * kcols:(n + 1) * kcols] = (dot(dscore, k) * QSCALE).astype(BF16)
             dv = dv + dot(weights16, g, ((0,), (0,)))
         DV[at, :] = dv.astype(BF16)
 
@@ -626,7 +631,7 @@
             collective_id=0, has_side_effects=True, vmem_limit_bytes=56 * 1024 * 1024
         ),
     )(
-        tokens.reshape(tok, feats), trace_index, input_norm_scale.reshape(1, feats),
+        tokens.reshape(tok, feats), trace_index, input_norm_scale,
         query_weight, key_weight, value_weight,
         query_down_weight.T, query_up_weight, value_down_weight.T, value_up_weight,
         output_gradient.reshape(tok, output_gradient.shape[2]),

time: 86.1 us -> 84.4 us (0.980)
  local copies, waits for them, and re-layouts: 1.29 us -> 0 us
where the time goes in v3:
time: 84.4 us; the launch traced here: 84.2 us
  Pallas kernels  83.5 us (99%)
    pallas_call x1, Pallas kernels, on_plane(): pl.pallas_call(functools.partial(plane_kernel, chain, coefficient), out_s...  81.8 us
    pallas_call x1, Pallas kernels, on_plane(): pl.pallas_call(unpack_kernel, out_shape=(jax.ShapeDtypeStruct((ranks, fea...  1.78 us

profile of v3, /device:TPU:0, one launch (start us, length us, event | category | flops | bytes accessed | tf_op | source)
XLA Modules:
  0.0 84.2 jit_solution(10877078190160230012)
XLA Ops:
  0.6 81.8 %shard_map.138.gathered = bf16[8,48,384]{2,1,0:T(8,128)(2,1)} custom-call(bf16[128,3072]{1,0:T(8,128)(2,1)} %bitcast.6, s32[1,128]{1,0:T(1,128)} %seg.1, bf16[3072]{0:T(1024)(128)(2,1)} %gain.1, bf16[192,2048]{1,0:T(8,128)(2,1)} %wq.1, bf16[192,1024]{1,0:T(8,128)(2,1)} %wk.1, bf16[192,1024]{1,0:T(8,128)(2,1)} %wv.1, bf16[16,3072]{1,0:T(8,128)(2,1)} %bitcast.8, ...), custom_call_target="tpu_custom_call" | custom-call | tf_op jit(solution)/shard_map/pallas_call | solution.py:604
  82.4 1.8 %shard_map.139 = (f32[16,3072]{1,0:T(8,128)}, f32[16,2048]{1,0:T(8,128)}, f32[16,3072]{1,0:T(8,128)}, f32[16,1024]{1,0:T(8,128)}) custom-call(bf16[8,48,384]{2,1,0:T(8,128)(2,1)} %shard_map.138.gathered), custom_call_target="tpu_custom_call" | custom-call | tf_op jit(solution)/shard_map/pallas_call | solution.py:639
